TPU v7x, 32 devices: a whole 2x2x4 slice. The times are simulated.
32 devices in a mesh: groups: 2 (over x), dp: 8 (over z, y), tensor: 2 (over core).
Axes of the slice: x: 2, y: 2, z: 4, core: 2. Of those that a mesh axis runs over, the one named last changes fastest.
Arguments:
- queries: bfloat16 [4096, 4096], P(('groups', 'dp'), 'tensor'), parts along dimension 0, may hold values from -6.5 to 6.5
- fresh_keys: bfloat16 [4096, 512], P(('groups', 'dp'), 'tensor'), parts along dimension 0, may hold values from -4 to 4
- fresh_values: bfloat16 [4096, 512], P(('groups', 'dp'), 'tensor'), parts along dimension 0, may hold values from -4 to 4
- key_pool_pages: bfloat16 [160, 128, 512], P(('groups', 'dp'), None, 'tensor'), parts along dimension 0, may hold values from -4 to 4
- value_pool_pages: bfloat16 [160, 128, 512], P(('groups', 'dp'), None, 'tensor'), parts along dimension 0, may hold values from -4 to 4
- block_table: int32 [16, 8], P(('groups', 'dp')), parts along dimension 0, may hold values from 0 to 9, as said below
- prefix_lengths: int32 [16], P('groups'), parts along dimension 0, may hold values from 0 to 1024, as said below
- out_weight: bfloat16 [4096, 4096], P('tensor', 'dp'), may hold values from -0.09375 to 0.09375
Outputs:
- output: bfloat16 [4096, 4096], P(('groups', 'dp'), 'tensor'), parts along dimension 0
There are 2 independent parts, one for each index of `groups`. A program takes and returns all parts, laid end to end along the dimension named above; an argument that names none is the same for every part. Nothing has to cross between parts.
Inputs may be any that keep to these rules, and one draw needn't show every extreme that they name: `block_table`: each row holds distinct pages of the request's own pool of 10 pages. `prefix_lengths`: some request has exactly 1024 cached tokens and some has none.
All inputs are finite; a program needn't handle non-finite values.
Results may differ from a plain program's by a relative error of at most 0.0095.
Values may be sent and summed in bfloat16 or wider, within the bound.
A program may use at most 128 MiB of HBM per device.

v0:
```python
import jax
import jax.numpy as jnp
from jax import lax
from jax.sharding import PartitionSpec as P

HEAD_SIZE = 128
QUERY_GROUP = 8
PAGE_TOKENS = 128
BLOCK_PAGES = 4


masked_score = -1e30


def starting(kv_heads, row_count):
    return (
        jnp.full((kv_heads, row_count), masked_score, jnp.float32),
        jnp.zeros((kv_heads, row_count), jnp.float32),
        jnp.zeros((kv_heads, row_count, HEAD_SIZE), jnp.float32),
    )


def attend(running, q_rows, key_block, values, visible):
    best_score, weight_sum, weighted = running
    scores = jnp.einsum(
        "krd,nkd->krn", q_rows, key_block, preferred_element_type=jnp.float32
    ) * HEAD_SIZE ** (-0.5)
    scores = jnp.where(visible, scores, masked_score)
    new_best = jnp.maximum(best_score, scores.max(-1))
    factor = jnp.exp(best_score - new_best)
    weights = jnp.where(visible, jnp.exp(scores - new_best[..., None]), 0.0)
    weight_sum = weight_sum * factor + weights.sum(-1)
    weighted = weighted * factor[..., None] + jnp.einsum(
        "krn,nkd->krd", weights.astype(jnp.bfloat16), values, preferred_element_type=jnp.float32
    )
    return (new_best, weight_sum, weighted)


def prefix_blocks(running, q_rows, reader, first_pos, key_limit, block_count):
    block_keys = BLOCK_PAGES * PAGE_TOKENS

    def advance(block_index, current):
        key_block, values = reader(block_index)
        position = first_pos + block_index * block_keys + jnp.arange(block_keys, dtype=jnp.int32)
        visible = (position < key_limit)[None, None, :]
        return attend(current, q_rows, key_block, values, visible)

    return lax.fori_loop(0, block_count, advance, running)


def pool_reader(key_pool_pages, value_pool_pages, request_pages, kv_heads):
    block_keys = BLOCK_PAGES * PAGE_TOKENS

    def reader(block_index):
        chosen = lax.dynamic_slice_in_dim(request_pages, block_index * BLOCK_PAGES, BLOCK_PAGES)
        key_block = jnp.take(key_pool_pages, chosen, axis=0).reshape(
            block_keys, kv_heads, HEAD_SIZE
        )
        values = jnp.take(value_pool_pages, chosen, axis=0).reshape(block_keys, kv_heads, HEAD_SIZE)
        return (key_block, values)

    return reader


def span_part(running, q_rows, fresh_keys, fresh_values, kv_heads):
    span_len = fresh_keys.shape[0]
    key_block = fresh_keys.reshape(span_len, kv_heads, HEAD_SIZE)
    values = fresh_values.reshape(span_len, kv_heads, HEAD_SIZE)
    token_index = jnp.arange(q_rows.shape[1], dtype=jnp.int32) % span_len
    visible = (jnp.arange(span_len, dtype=jnp.int32)[None, :] <= token_index[:, None])[None]
    return attend(running, q_rows, key_block, values, visible)


def to_rows(queries, kv_heads):
    span_len = queries.shape[0]
    return (
        queries.reshape(span_len, kv_heads, QUERY_GROUP, HEAD_SIZE)
        .transpose(1, 2, 0, 3)
        .reshape(kv_heads, QUERY_GROUP * span_len, HEAD_SIZE)
    )


def shards(
    queries,
    fresh_keys,
    fresh_values,
    key_pool_pages,
    value_pool_pages,
    block_table,
    prefix_lengths,
    out_weight,
):
    span_len = queries.shape[0]
    kv_heads = fresh_keys.shape[1] // HEAD_SIZE
    row_count = QUERY_GROUP * span_len
    block_keys = BLOCK_PAGES * PAGE_TOKENS
    q_rows = to_rows(queries, kv_heads)
    initial = starting(kv_heads, row_count)
    own_index = lax.axis_index("dp")
    own_length = prefix_lengths[own_index]
    request_pages = block_table[0]
    own_reader = pool_reader(key_pool_pages, value_pool_pages, request_pages, kv_heads)
    running = prefix_blocks(
        initial, q_rows, own_reader, 0, own_length, (own_length + block_keys - 1) // block_keys
    )
    running = span_part(running, q_rows, fresh_keys, fresh_values, kv_heads)
    best_score, weight_sum, weighted = running
    attended = (weighted / weight_sum[..., None]).reshape(
        kv_heads, QUERY_GROUP, span_len, HEAD_SIZE
    )
    attended = (
        attended.transpose(2, 0, 1, 3)
        .reshape(span_len, kv_heads * QUERY_GROUP * HEAD_SIZE)
        .astype(jnp.bfloat16)
    )
    columns = jnp.dot(
        attended,
        lax.all_gather(out_weight, "dp", axis=1, tiled=True),
        preferred_element_type=jnp.float32,
    )
    return lax.psum_scatter(columns.astype(jnp.bfloat16), "tensor", scatter_dimension=1, tiled=True)


def solution(mesh):
    return jax.shard_map(
        shards,
        mesh=mesh,
        in_specs=(
            P(("groups", "dp"), "tensor"),
            P(("groups", "dp"), "tensor"),
            P(("groups", "dp"), "tensor"),
            P(("groups", "dp"), None, "tensor"),
            P(("groups", "dp"), None, "tensor"),
            P(("groups", "dp"), None),
            P("groups"),
            P("tensor", "dp"),
        ),
        out_specs=P(("groups", "dp"), "tensor"),
        check_vma=False,
    )
```

profile of v0, /device:TPU:24, one launch (start us, length us, event | category | flops | bytes accessed | tf_op | source)
XLA Modules:
  0.0 264.4 jit_solution(9661835527707682932)
XLA Ops:
  6.5 0.0 copy-start
  6.5 0.0 all-gather.2.cloned.1.call-start
  6.5 0.7 all-gather.2.cloned.1.call-update
  7.3 0.0 reduce-scatter.2.cloned.1.call-start
  7.3 1.3 dynamic_slice.6
  9.3 1.5 copy.28
  10.7 0.3 copy.19
  11.0 0.0 copy-start.3
  11.0 0.3 iota_compare_fusion
  11.3 0.0 copy-done
  11.4 2.9 %fusion.17 = (f32[2,2048]{1,0:T(2,128)S(1)}, f32[2,2048,256]{1,2,0:T(8,128)}) fusion(pred[2048,256]{0,1:T(8,128)(4,1)S(1)} %iota_compare_fusion, bf16[2,2048,128]{2,1,0:T(8,128)(2,1)S(1)} %bitcast.54, bf16[256,256]{1,0:T(8,128)(2,1)S(1)} %copy-done), kind=kOutput, calls=%fused_computation.30 | convolution fusion | flops 271577088 | bytes 5914624 | tf_op jit(solution)/shard_map/krd,nkd->krn/dot_general | solution.py:25
  14.3 1.5 broadcast_in_dim.69
  15.8 0.0 copy-done.3
  15.8 34.8 %while.14 = (s32[]{:T(128)}, f32[2,2048]{1,0:T(2,128)S(1)}, f32[2,2048]{1,0:T(2,128)S(1)}, f32[2,2048,128]{2,1,0:T(8,128)}, s32[]{:T(128)}, /*index=5*/s32[]{:T(...) while((s32[]{:T(128)}, f32[2,2048]{1,0:T(2,128)S(1)}, ...), condition=%wide.region_3.5_spmd, body=%wide.region_0.4_spmd.sunk | while | flops 1102325760 | bytes 67901768 | solution.py:48
  15.8 0.1 compare_and_fusion.2
  15.9 1.7 gather_fusion
  17.5 1.8 gather_fusion.1
  19.3 0.1 broadcast_select_fusion.3
  19.4 0.1 reshape.101
  19.5 0.6 add_compare_fusion.2
  20.1 1.4 bitcast_reduce_fusion.2
  21.5 0.0 copy-start.1
  21.5 2.6 fusion.53
  24.1 0.6 copy-done.1
  24.8 0.1 reshape.102
  24.8 8.5 %fusion.54 = f32[2,2048,128]{2,1,0:T(8,128)} fusion(f32[2,512,2048]{2,1,0:T(8,128)} %copy-done.1, f32[2,2048]{1,0:T(2,128)S(1)} %max.8, pred[512]{0:T(512)(128)(4,1)S(1)} %add_compare_fusion.2, f32[2,2048,128]{2,1,0:T(8,128)} %get-tuple-element.192, f32[2,2048]{1,0:T(2,128)S(1)} %get-tuple-element.172, bf16[512,2,128]{2,1,0:T(2,128)(2,1)S(1)} %reshape.102), kind=kOutput, calls=%fused_computation.12.clone.1 | convolution fusion | flops 548405248 | bytes 12878336 | tf_op jit(solution)/shard_map/while/body/krn,nkd->krd/dot_general | solution.py:33
  33.3 0.1 compare_and_fusion.2
  33.4 1.7 gather_fusion
  35.1 1.7 gather_fusion.1
  36.7 0.1 broadcast_select_fusion.3
  36.8 0.1 reshape.101
  36.9 0.6 add_compare_fusion.2
  37.5 1.4 bitcast_reduce_fusion.2
  38.9 0.0 copy-start.1
  38.9 2.6 fusion.53
  41.5 0.6 copy-done.1
  42.2 0.1 reshape.102
  42.2 8.3 %fusion.54 = f32[2,2048,128]{2,1,0:T(8,128)} fusion(f32[2,512,2048]{2,1,0:T(8,128)} %copy-done.1, f32[2,2048]{1,0:T(2,128)S(1)} %max.8, pred[512]{0:T(512)(128)(4,1)S(1)} %add_compare_fusion.2, f32[2,2048,128]{2,1,0:T(8,128)} %get-tuple-element.192, f32[2,2048]{1,0:T(2,128)S(1)} %get-tuple-element.172, bf16[512,2,128]{2,1,0:T(2,128)(2,1)S(1)} %reshape.102), kind=kOutput, calls=%fused_computation.12.clone.1 | convolution fusion | flops 548405248 | bytes 12878336 | tf_op jit(solution)/shard_map/while/body/krn,nkd->krd/dot_general | solution.py:33
  50.6 0.0 copy-start.2
  50.6 3.5 %fusion.18 = f32[2,2048]{1,0:T(2,128)S(1)} fusion(f32[2,2048,256]{1,2,0:T(8,128)} %get-tuple-element.95, f32[2,2048]{1,0:T(2,128)S(1)} %max.6, pred[2048,256]{0,1:T(8,128)(4,1)S(1)} %iota_compare_fusion), kind=kLoop, calls=%fused_computation.31 | loop fusion | flops 5238784 | bytes 4751360 | tf_op jit(solution)/shard_map/reduce_sum | solution.py:32
  54.1 0.0 copy-done.2
  54.1 0.0 copy-done.4
  54.1 4.2 %fusion.21 = bf16[2,2048,128]{2,1,0:T(8,128)(2,1)S(1)} fusion(f32[2,2048,256]{1,2,0:T(8,128)S(1)} %copy-done.2, f32[2,2048]{1,0:T(2,128)S(1)} %max.6, f32[2,2048,128]{2,1,0:T(8,128)} %get-tuple-element.61, pred[2048,256]{0,1:T(8,128)(4,1)S(1)} %iota_compare_fusion, f32[2,2048]{1,0:T(2,128)S(1)} %get-tuple-element.88, f32[2,2048]{1,0:T(2,128)S(1)} %get-tuple-element.89, ...), kind=kOutput, calls=%fused_computation.35 | convolution fusion | flops 275775488 | bytes 8044544 | tf_op jit(solution)/shard_map/krn,nkd->krd/dot_general | solution.py:33
  58.4 0.5 copy.23
  58.9 176.9 %all-gather.2.cloned.1.call-done = bf16[2048,4096]{1,0:T(8,128)(2,1)} async-done(((bf16[2048,512]{1,0:T(8,128)(2,1)}), bf16[2048,4096]{1,0:T(8,128)(2,1)}) %all-gather.2.cloned.1.call-update) | async-done | bytes 16777232 | tf_op jit(solution)/shard_map/all_gather | solution.py:118
  235.8 11.5 %convolution_convert_fusion = bf16[256,4096]{1,0:T(8,128)(2,1)} fusion(bf16[256,2048]{0,1:T(8,128)(2,1)S(1)} %bitcast.56, bf16[2048,4096]{1,0:T(8,128)(2,1)} %all-gather.2.cloned.1.call-done), kind=kOutput, calls=%fused_computation.27 | convolution fusion | flops 4296015872 | bytes 19922944 | tf_op jit(solution)/shard_map/dot_general | solution.py:116
  247.3 0.0 reduce-scatter.2.cloned.1.call-update
  247.3 10.2 %reduce-scatter.2.cloned.1.call-done = bf16[256,2048]{1,0:T(8,128)(2,1)} async-done(((bf16[256,4096]{1,0:T(8,128)(2,1)}), bf16[256,2048]{1,0:T(8,128)(2,1)}) %reduce-scatter.2.cloned.1.call-update) | async-done | bytes 1048592 | tf_op jit(solution)/shard_map/reduce_scatter | solution.py:121
  (14 shorter events, 0.2 us)
Async XLA Ops:
  6.5 4.8 %copy-start = (bf16[256,256]{1,0:T(8,128)(2,1)S(1)}, bf16[256,256]{1,0:T(8,128)(2,1)}, u32[]{:S(2)}) copy-start(bf16[256,256]{1,0:T(8,128)(2,1)} %param.13) | copy-start | bytes 393220
  6.5 229.2 %all-gather.2.cloned.1.call-start = ((), (), s32[]{:S(2)}) async-start(), calls=%async_computation.1 | async-start | bytes 18874368 | tf_op jit(solution)/shard_map/all_gather | solution.py:118
  7.3 250.3 %reduce-scatter.2.cloned.1.call-start = ((), (), s32[]{:S(2)}) async-start(), calls=%async_computation.2 | async-start | bytes 3145728 | tf_op jit(solution)/shard_map/reduce_scatter | solution.py:121
  11.0 4.7 %copy-start.3 = (s32[1,8]{1,0:T(1,128)S(1)}, s32[1,8]{1,0:T(1,128)}, u32[]{:S(2)}) copy-start(s32[1,8]{1,0:T(1,128)} %param.17) | copy-start | bytes 100
  21.5 3.2 %copy-start.1 = (f32[2,512,2048]{2,1,0:T(8,128)}, f32[2,512,2048]{2,1,0:T(8,128)S(1)}, u32[]{:S(2)}) copy-start(f32[2,512,2048]{2,1,0:T(8,128)S(1)} %get-tuple-element.170) | copy-start | bytes 25165828 | tf_op jit(solution)/shard_map/while
  38.9 3.2 %copy-start.1 = (f32[2,512,2048]{2,1,0:T(8,128)}, f32[2,512,2048]{2,1,0:T(8,128)S(1)}, u32[]{:S(2)}) copy-start(f32[2,512,2048]{2,1,0:T(8,128)S(1)} %get-tuple-element.170) | copy-start | bytes 25165828 | tf_op jit(solution)/shard_map/while
  50.6 3.6 %copy-start.2 = (f32[2,2048,256]{1,2,0:T(8,128)S(1)}, f32[2,2048,256]{1,2,0:T(8,128)}, u32[]{:S(2)}) copy-start(f32[2,2048,256]{1,2,0:T(8,128)} %get-tuple-element.95) | copy-start | bytes 12582916
  50.6 3.6 %copy-start.4 = (bf16[256,256]{1,0:T(8,128)(2,1)S(1)}, bf16[256,256]{1,0:T(8,128)(2,1)}, u32[]{:S(2)}) copy-start(bf16[256,256]{1,0:T(8,128)(2,1)} %param.14) | copy-start | bytes 393220
Sparse Core Ops, SparseCore 0:
  9.4 226.3 all-gather.1
  247.5 10.0 reduce-scatter.1
where the time goes:
time: 266 us; the launch traced here: 264 us
  waiting for transfers between devices  188 us (71%)
  matrix products  38.2 us (14%)
  between operations  14.2 us (5%)
  local copies, waits for them, and re-layouts  13.3 us (5%)
  other arithmetic  10.7 us (4%)
    all_gather x1, waiting for transfers between devices, shards(): lax.all_gather(out_weight, 'dp', axis=1, tiled=True)  177 us
    dot_general x3, matrix products, attend(): jnp.einsum('krn,nkd->krd', weights.astype(jnp.bfloat16), values, preferre...  21 us
    dot_general x1, matrix products, shards(): jnp.dot(attended, lax.all_gather(out_weight, 'dp', axis=1, tiled=True), p...  11.5 us
    reduce_scatter x1, waiting for transfers between devices, shards(): lax.psum_scatter(columns.astype(jnp.bfloat16), 'tensor', scatter_dimensio...  10.2 us
    reduce_sum x3, other arithmetic, attend(): weight_sum = weight_sum * factor + weights.sum(-1)  8.61 us
    dot_general x3, matrix products, attend(): jnp.einsum('krd,nkd->krn', q_rows, key_block, preferred_element_type=jnp....  5.65 us
  transfers between devices with their start and end apart: 2, of which 2 were waited for; matrix products, arithmetic and copies ran while one was open for 19% of the time, Pallas kernels for 0%

commit v1 on v0

v1 whole, which is shorter than its diff:
```python
import functools

import jax
import jax.numpy as jnp
from jax import lax
from jax.experimental import pallas as pl
from jax.experimental.pallas import tpu as pltpu
from jax.sharding import PartitionSpec as P

HEAD_SIZE = 128
QUERY_GROUP = 8
PAGE_TOKENS = 128
CHUNK = 256
SCALE = HEAD_SIZE ** (-0.5) * 1.4426950408889634
MASKED = -1e30


def kernel(
    line, q_ref, fk_ref, fv_ref, kp_ref, vp_ref, table_ref, len_ref, w_ref, out_ref,
    wbuf, act, stage, keys, values, bias,
    w_recv, w_next, w_side, own_send, act_recv, act_send, act_fwd, out_send, out_recv,
):
    group, dp, core = lax.axis_index("groups"), lax.axis_index("dp"), lax.axis_index("tensor")
    z, y = dp // 2, dp % 2
    half = group % 2
    cousin = group + 1 - 2 * half
    other = 1 - core
    peer = z * 2 + 1 - y
    shards = line // 2
    part, cols = w_ref.shape
    tokens = q_ref.shape[0]
    per_core = part // CHUNK
    per_half = per_core // 2
    own_core = z // shards
    own_slot = z - own_core * shards
    wide = act.shape[2] // 2
    step_cols = wide // per_core
    heads_per_step = step_cols // HEAD_SIZE
    heads_per_kv = QUERY_GROUP
    tile = min(cols, 256)
    tiles = cols // tile

    def remote(src, dst, send, recv, where):
        return pltpu.make_async_remote_copy(
            src_ref=src, dst_ref=dst, send_sem=send, recv_sem=recv,
            device_id=where, device_id_type=pl.DeviceIdType.MESH,
        )

    def rows(k):
        return pl.ds(pl.multiple_of(k * CHUNK, CHUNK), CHUNK)

    barrier = pltpu.get_barrier_semaphore()

    def greet(where):
        pl.semaphore_signal(barrier, inc=1, device_id=where, device_id_type=pl.DeviceIdType.MESH)

    greet((group, dp, other))
    greet((cousin, dp, core))
    greet((group, peer, core))

    @pl.when(z > 0)
    def _():
        greet((group, dp - 2, core))
        greet((group, dp - 2, other))

    @pl.when(z < line - 1)
    def _():
        greet((group, dp + 2, core))
        greet((group, dp + 2, other))

    neighbours = jnp.where(z > 0, 2, 0) + jnp.where(z < line - 1, 2, 0)
    pl.semaphore_wait(barrier, 3 + neighbours)

    def own_copy(k, side):
        slab = core * per_core + k
        where = (group, dp + 2 * side, own_core) if side else (group, dp, other)
        return remote(
            w_ref.at[rows(k)], wbuf.at[own_slot, rows(slab)],
            own_send.at[side + 1, k], w_recv.at[own_slot, slab], where,
        )

    def own_local(k):
        slab = core * per_core + k
        return pltpu.make_async_copy(
            w_ref.at[rows(k)], wbuf.at[own_slot, rows(slab)], w_recv.at[own_slot, slab]
        )

    def each_own(act_on):
        def one(j, carry):
            k = half * per_half + j

            @pl.when(z > 0)
            def _():
                act_on(own_copy(k, -1))

            @pl.when(z < line - 1)
            def _():
                act_on(own_copy(k, 1))

            return carry

        lax.fori_loop(0, per_half, one, 0)

        @pl.when(core != own_core)
        def _():
            lax.fori_loop(0, per_core, lambda k, carry: (act_on(own_copy(k, 0)), carry)[1], 0)

    each_own(lambda copy: copy.start())

    @pl.when(core == own_core)
    def _():
        lax.fori_loop(0, per_core, lambda k, carry: (own_local(k).start(), carry)[1], 0)

    def slab_of(i, which):
        return (i % 2) * per_core + which * per_half + i // 2

    def landed(slot, slab):
        remote(
            wbuf.at[slot, rows(slab)], wbuf.at[slot, rows(slab)],
            w_next.at[slot, slab], w_recv.at[slot, slab], (group, dp, other),
        ).wait_recv()

    def next_copy(slot, slab, step):
        return remote(
            wbuf.at[slot, rows(slab)], wbuf.at[slot, rows(slab)],
            w_next.at[slot, slab], w_recv.at[slot, slab], (group, dp + 2 * step, core),
        )

    def side_copy(slot, slab):
        return remote(
            wbuf.at[slot, rows(slab)], wbuf.at[slot, rows(slab)],
            w_side.at[slot, slab], w_recv.at[slot, slab], (cousin, dp, core),
        )

    def pass_on(slot, origin, i):
        slab = slab_of(i, half)
        landed(slot, slab)

        @pl.when(jnp.logical_and(origin < z, z < line - 1))
        def _():
            next_copy(slot, slab, 1).start()

        @pl.when(jnp.logical_and(origin > z, z > 0))
        def _():
            next_copy(slot, slab, -1).start()

        side_copy(slot, slab).start()

    length = len_ref[dp]
    cached = table_ref.shape[1] * PAGE_TOKENS
    for j in range(table_ref.shape[1]):
        page = table_ref[0, j]
        keys[j * PAGE_TOKENS:(j + 1) * PAGE_TOKENS, :] = kp_ref[page]
        values[j * PAGE_TOKENS:(j + 1) * PAGE_TOKENS, :] = vp_ref[page]
    keys[cached:, :] = fk_ref[...]
    values[cached:, :] = fv_ref[...]
    position = lax.broadcasted_iota(jnp.int32, (tokens, cached), 1)
    bias[:, :cached] = jnp.where(position < length, 0.0, MASKED)
    bias[:, cached:] = jnp.where(
        lax.broadcasted_iota(jnp.int32, (tokens, tokens), 1)
        <= lax.broadcasted_iota(jnp.int32, (tokens, tokens), 0),
        0.0, MASKED,
    )

    def act_cols(slab):
        return pl.ds(pl.multiple_of(slab * step_cols, step_cols), step_cols)

    def act_copy(i, to_peer):
        slab = core * per_core + i
        src = act.at[0, :, act_cols(slab)]
        if to_peer:
            return remote(src, act.at[1, :, act_cols(slab)], act_send.at[1, i],
                          act_recv.at[1, slab], (group, peer, core))
        return remote(src, src, act_send.at[0, i], act_recv.at[0, slab], (group, dp, other))

    def act_forward(i):
        slab = core * per_core + i
        ref = act.at[1, :, act_cols(slab)]
        return remote(ref, ref, act_fwd.at[i], act_recv.at[1, slab], (group, dp, other))

    def act_landed(block, slab):
        ref = act.at[block, :, act_cols(slab)]
        remote(ref, ref, act_fwd.at[0], act_recv.at[block, slab], (group, dp, other)).wait_recv()

    def relay(i):
        act_landed(1, core * per_core + i)
        act_forward(i).start()

    lag = 2

    def attention_step(i, carry):
        kv = (i * heads_per_step) // heads_per_kv
        kv_cols = pl.ds(pl.multiple_of(kv * HEAD_SIZE, HEAD_SIZE), HEAD_SIZE)
        for n in range(heads_per_step):
            head = i * heads_per_step + n
            q = q_ref[:, pl.ds(pl.multiple_of(head * HEAD_SIZE, HEAD_SIZE), HEAD_SIZE)]
            scores = lax.dot_general(
                q, keys[:, kv_cols], (((1,), (1,)), ((), ())), preferred_element_type=jnp.float32
            )
            scores = scores * SCALE + bias[...]
            weights = jnp.exp2(scores - jnp.max(scores, axis=-1, keepdims=True))
            total = jnp.sum(weights, axis=-1, keepdims=True)
            weighted = jnp.dot(
                weights.astype(jnp.bfloat16), values[:, kv_cols], preferred_element_type=jnp.float32
            )
            start = core * wide + head * HEAD_SIZE
            act[0, :, pl.ds(pl.multiple_of(start, HEAD_SIZE), HEAD_SIZE)] = (
                weighted / total
            ).astype(jnp.bfloat16)
        act_copy(i, True).start()
        act_copy(i, False).start()
        for side in (-1, 1):
            origin = z + side

            @pl.when(jnp.logical_and(
                jnp.logical_and(origin >= core * shards, origin < (core + 1) * shards), True))
            def _():
                pass_on(origin - core * shards, origin, i)

        @pl.when(i >= lag)
        def _():
            relay(i - lag)

        return carry

    lax.fori_loop(0, per_core, attention_step, 0)
    for i in range(per_core - lag, per_core):
        relay(i)

    def origin_of(p):
        low = core * shards
        inside = low + (z - low + p + shards * line) % shards
        return jnp.where(z < low, low + p, jnp.where(z >= low + shards, low + shards - 1 - p, inside))

    def out_cols(origin, n):
        start = (origin * 2 + y - core * 2 * shards) * cols + n * tile
        return pl.ds(pl.multiple_of(start, 128), tile)

    def out_copy(slot, n, column):
        return remote(
            stage.at[slot, n], out_ref.at[:, column], out_send.at[slot, n],
            out_recv.at[slot, n], (group, peer, core),
        )

    def product(block, slot, n):
        return jnp.dot(
            act[block], wbuf[slot, :, pl.ds(pl.multiple_of(n * tile, 128), tile)],
            preferred_element_type=jnp.float32,
        ).astype(jnp.bfloat16)

    def piece(origin, m):
        slot = origin - core * shards
        n = m % tiles
        column = out_cols(origin, n)

        @pl.when(m < tiles)
        def _():
            stage[slot, n] = product(1, slot, n)
            out_copy(slot, n, column).start()

        @pl.when(m >= tiles)
        def _():
            out_ref[:, column] = product(0, slot, n)

    def rest_landed(origin):
        slot = origin - core * shards

        def one(i, carry):
            landed(slot, slab_of(i, 1 - half))

            @pl.when(origin == z)
            def _():
                landed(slot, slab_of(i, half))

            return carry

        lax.fori_loop(0, per_core, one, 0)

    def acts_landed():
        def one(i, carry):
            act_landed(0, other * per_core + i)
            act_landed(1, other * per_core + i)
            return carry

        lax.fori_loop(0, per_core, one, 0)

    def shard_step(p, carry):
        origin = origin_of(p)
        before = origin_of(jnp.maximum(p - 1, 0))

        def chunk_step(i, inner):
            @pl.when(jnp.logical_or(origin > z + 1, origin < z - 1))
            def _():
                pass_on(origin - core * shards, origin, i)

            @pl.when(jnp.logical_and(p > 0, i == 1))
            def _():
                @pl.when(p == 1)
                def _():
                    acts_landed()

                rest_landed(before)

            @pl.when(jnp.logical_and(jnp.logical_and(p > 0, i % 2 == 1), i // 2 < 2 * tiles))
            def _():
                piece(before, i // 2)

            return inner

        lax.fori_loop(0, per_core, chunk_step, 0)
        return carry

    lax.fori_loop(0, shards, shard_step, 0)
    if shards == 1:
        acts_landed()
    last = origin_of(shards - 1)
    rest_landed(last)
    lax.fori_loop(0, 2 * tiles, lambda m, carry: (piece(last, m), carry)[1], 0)

    def finish(slot, carry):
        origin = core * shards + slot
        for n in range(tiles):
            start = (origin * 2 + 1 - y - core * 2 * shards) * cols + n * tile
            copy = out_copy(slot, n, pl.ds(pl.multiple_of(start, 128), tile))
            copy.wait_recv()
            copy.wait_send()

        @pl.when(origin != z)
        def _():
            def one(i, inner):
                slab = slab_of(i, half)

                @pl.when(jnp.logical_and(origin < z, z < line - 1))
                def _():
                    next_copy(slot, slab, 1).wait_send()

                @pl.when(jnp.logical_and(origin > z, z > 0))
                def _():
                    next_copy(slot, slab, -1).wait_send()

                side_copy(slot, slab).wait_send()
                return inner

            lax.fori_loop(0, per_core, one, 0)

        return carry

    lax.fori_loop(0, shards, finish, 0)

    def acts_sent(i, carry):
        act_copy(i, True).wait_send()
        act_copy(i, False).wait_send()
        act_forward(i).wait_send()
        return carry

    lax.fori_loop(0, per_core, acts_sent, 0)
    each_own(lambda copy: copy.wait_send())


def shards_program(line, queries, fresh_keys, fresh_values, key_pages, value_pages, table, lengths, weight):
    tokens, wide = queries.shape
    part, cols = weight.shape
    per_core = part // CHUNK
    shards = line // 2
    tile = min(cols, 256)
    tiles = cols // tile
    span = table.shape[1] * PAGE_TOKENS + tokens
    kv_width = fresh_keys.shape[1]
    out_width = 2 * shards * cols
    vmem = pl.BlockSpec(memory_space=pltpu.VMEM)
    smem = pl.BlockSpec(memory_space=pltpu.SMEM)
    dma = pltpu.SemaphoreType.DMA
    heads = wide // HEAD_SIZE
    flops = 4 * heads * tokens * span * HEAD_SIZE + 2 * 2 * tokens * 2 * part * shards * cols
    return pl.pallas_call(
        functools.partial(kernel, line),
        out_shape=jax.ShapeDtypeStruct((tokens, out_width), jnp.bfloat16),
        in_specs=[vmem, vmem, vmem, vmem, vmem, smem, smem, pl.BlockSpec(memory_space=pl.ANY)],
        out_specs=vmem,
        scratch_shapes=[
            pltpu.VMEM((shards, 2 * part, cols), jnp.bfloat16),
            pltpu.VMEM((2, tokens, 2 * wide), jnp.bfloat16),
            pltpu.VMEM((shards, tiles, tokens, tile), jnp.bfloat16),
            pltpu.VMEM((span, kv_width), jnp.bfloat16),
            pltpu.VMEM((span, kv_width), jnp.bfloat16),
            pltpu.VMEM((tokens, span), jnp.float32),
            dma((shards, 2 * per_core)),
            dma((shards, 2 * per_core)),
            dma((shards, 2 * per_core)),
            dma((3, per_core)),
            dma((2, 2 * per_core)),
            dma((2, per_core)),
            dma((per_core,)),
            dma((shards, tiles)),
            dma((shards, tiles)),
        ],
        compiler_params=pltpu.CompilerParams(
            collective_id=0, has_side_effects=True, vmem_limit_bytes=60 * 1024 * 1024
        ),
        cost_estimate=pl.CostEstimate(
            flops=flops, bytes_accessed=8 * 1024 * 1024, transcendentals=heads * tokens * span
        ),
    )(queries, fresh_keys, fresh_values, key_pages, value_pages, table, lengths, weight)


def solution(mesh):
    return jax.shard_map(
        functools.partial(shards_program, mesh.shape["dp"] // 2),
        mesh=mesh,
        in_specs=(
            P(("groups", "dp"), "tensor"),
            P(("groups", "dp"), "tensor"),
            P(("groups", "dp"), "tensor"),
            P(("groups", "dp"), None, "tensor"),
            P(("groups", "dp"), None, "tensor"),
            P(("groups", "dp"), None),
            P("groups"),
            P("tensor", "dp"),
        ),
        out_specs=P(("groups", "dp"), "tensor"),
        check_vma=False,
    )
```

time: 266 us -> 95.3 us (0.36)
  waiting for transfers between devices: 188 us -> 0 us
  Pallas kernels: 0 us -> 92.8 us
  matrix products: 38.2 us -> 0 us
  between operations: 14.2 us -> 0.01 us
  local copies, waits for them, and re-layouts: 13.3 us -> 2.3 us
  other arithmetic: 10.7 us -> 0 us
    all_gather x1 -> x0, waiting for transfers between devices: 177 us -> none  [shards(): lax.all_gather(out_weight, 'dp', axis=1, tiled=True)]
    pallas_call x0 -> x1, Pallas kernels: none -> 92.8 us  [shards_program(): pl.pallas_call(functools.partial(kernel, line), out_shape=jax.ShapeDtypeS...]
    dot_general x7 -> x0, matrix products: 38.2 us -> none  [the longest x3 21 us: attend(): jnp.einsum('krn,nkd->krd', weights.astype(jnp.bfloat16), values, preferre...]
    reduce_scatter x1 -> x0, waiting for transfers between devices: 10.2 us -> none  [shards(): lax.psum_scatter(columns.astype(jnp.bfloat16), 'tensor', scatter_dimensio...]
    reduce_sum x3 -> x0, other arithmetic: 8.61 us -> none  [attend(): weight_sum = weight_sum * factor + weights.sum(-1)]
    gather x4 -> x0, local copies, waits for them, and re-layouts: 6.71 us -> none  [the longest x2 3.41 us: reader(): jnp.take(key_pool_pages, chosen, axis=0)]
  transfers between devices with their start and end apart: 2 -> 0, of which waited for: 2 -> 0; matrix products, arithmetic and copies ran while one was open for 19% -> 0% of each run, Pallas kernels for 0% -> 0%
where the time goes in v1:
time: 95.3 us; the launch traced here: 95.1 us
  Pallas kernels  92.8 us (97%)
  local copies, waits for them, and re-layouts  2.3 us (2%)
    pallas_call x1, Pallas kernels, shards_program(): pl.pallas_call(functools.partial(kernel, line), out_shape=jax.ShapeDtypeS...  92.8 us
    unnamed x1, local copies, waits for them, and re-layouts  2.3 us

profile of v1, /device:TPU:24, one launch (start us, length us, event | category | flops | bytes accessed | tf_op | source)
XLA Modules:
  0.0 95.1 jit_solution(12516535904659392923)
XLA Ops:
  0.0 92.8 %shard_map.82 = bf16[256,2048]{1,0:T(8,128)(2,1)} custom-call(bf16[256,2048]{1,0:T(8,128)(2,1)} %q_ref.1, bf16[256,256]{1,0:T(8,128)(2,1)} %fk_ref.1, bf16[256,256]{1,0:T(8,128)(2,1)} %fv_ref.1, bf16[10,128,256]{2,1,0:T(8,128)(2,1)} %kp_ref.1, bf16[10,128,256]{2,1,0:T(8,128)(2,1)} %vp_ref.1, s32[1,8]{1,0:T(1,128)} %table_ref.1, s32[8]{0:T(128)} %len_ref.1, ...), custom_call_target="tpu_custom_call" | custom-call | flops 6979321856 | bytes 8388608 | tf_op jit(solution)/shard_map/pallas_call | solution.py:375
  92.8 2.3 %copy.10 = bf16[256,2048]{1,0:T(8,128)(2,1)} copy(bf16[256,2048]{1,0:T(8,128)(2,1)} %shard_map.82) | data formatting | bytes 2097152

commit v2 on v1

--- a/solution.py
+++ b/solution.py
@@ -18,27 +18,29 @@
 def kernel(
     line, q_ref, fk_ref, fv_ref, kp_ref, vp_ref, table_ref, len_ref, w_ref, out_ref,
     wbuf, act, stage, keys, values, bias,
-    w_recv, w_next, w_side, own_send, act_recv, act_send, act_fwd, out_send, out_recv,
+    w_recv, w_next, w_x, w_y, own_send, act_recv, act_send, act_fwd, out_send, out_recv,
 ):
     group, dp, core = lax.axis_index("groups"), lax.axis_index("dp"), lax.axis_index("tensor")
     z, y = dp // 2, dp % 2
-    half = group % 2
+    half, parity = group % 2, z % 2
     cousin = group + 1 - 2 * half
     other = 1 - core
-    peer = z * 2 + 1 - y
-    shards = line // 2
+    beside = z * 2 + 1 - y
+    peer = (z + 1 - 2 * parity) * 2 + y
+    span = line // 2
+    planes = span // 2
     part, cols = w_ref.shape
     tokens = q_ref.shape[0]
     per_core = part // CHUNK
     per_half = per_core // 2
-    own_core = z // shards
-    own_slot = z - own_core * shards
+    own_core = z // span
     wide = act.shape[2] // 2
     step_cols = wide // per_core
     heads_per_step = step_cols // HEAD_SIZE
     heads_per_kv = QUERY_GROUP
     tile = min(cols, 256)
     tiles = cols // tile
+    over_y = per_core * 5 // 8
 
     def remote(src, dst, send, recv, where):
         return pltpu.make_async_remote_copy(
@@ -49,6 +51,9 @@
     def rows(k):
         return pl.ds(pl.multiple_of(k * CHUNK, CHUNK), CHUNK)
 
+    def slot_of(origin, side):
+        return (origin % span // 2) * 2 + side
+
     barrier = pltpu.get_barrier_semaphore()
 
     def greet(where):
@@ -57,43 +62,51 @@
     greet((group, dp, other))
     greet((cousin, dp, core))
     greet((group, peer, core))
-
-    @pl.when(z > 0)
+    greet((group, beside, core))
+    greet((group, beside, other))
+
+    @pl.when(z > 1)
     def _():
-        greet((group, dp - 2, core))
-        greet((group, dp - 2, other))
-
-    @pl.when(z < line - 1)
+        greet((group, dp - 4, core))
+        greet((group, dp - 4, other))
+
+    @pl.when(z < line - 2)
     def _():
-        greet((group, dp + 2, core))
-        greet((group, dp + 2, other))
-
-    neighbours = jnp.where(z > 0, 2, 0) + jnp.where(z < line - 1, 2, 0)
-    pl.semaphore_wait(barrier, 3 + neighbours)
-
-    def own_copy(k, side):
+        greet((group, dp + 4, core))
+        greet((group, dp + 4, other))
+
+    neighbours = jnp.where(z > 1, 2, 0) + jnp.where(z < line - 2, 2, 0)
+    pl.semaphore_wait(barrier, 5 + neighbours)
+
+    def own_copy(k, way):
         slab = core * per_core + k
-        where = (group, dp + 2 * side, own_core) if side else (group, dp, other)
+        where = (
+            (group, dp - 4, own_core), (group, dp + 4, own_core),
+            (group, beside, own_core), (group, dp, other),
+        )[way]
+        slot = slot_of(z, y)
         return remote(
-            w_ref.at[rows(k)], wbuf.at[own_slot, rows(slab)],
-            own_send.at[side + 1, k], w_recv.at[own_slot, slab], where,
+            w_ref.at[rows(k)], wbuf.at[slot, rows(slab)],
+            own_send.at[way, k], w_recv.at[slot, slab], where,
         )
 
     def own_local(k):
         slab = core * per_core + k
+        slot = slot_of(z, y)
         return pltpu.make_async_copy(
-            w_ref.at[rows(k)], wbuf.at[own_slot, rows(slab)], w_recv.at[own_slot, slab]
+            w_ref.at[rows(k)], wbuf.at[slot, rows(slab)], w_recv.at[slot, slab]
         )
 
     def each_own(act_on):
         def one(j, carry):
             k = half * per_half + j
-
-            @pl.when(z > 0)
-            def _():
-                act_on(own_copy(k, -1))
-
-            @pl.when(z < line - 1)
+            act_on(own_copy(k, 2))
+
+            @pl.when(z > 1)
+            def _():
+                act_on(own_copy(k, 0))
+
+            @pl.when(z < line - 2)
             def _():
                 act_on(own_copy(k, 1))
 
@@ -103,7 +116,7 @@
 
         @pl.when(core != own_core)
         def _():
-            lax.fori_loop(0, per_core, lambda k, carry: (act_on(own_copy(k, 0)), carry)[1], 0)
+            lax.fori_loop(0, per_core, lambda k, carry: (act_on(own_copy(k, 3)), carry)[1], 0)
 
     each_own(lambda copy: copy.start())
 
@@ -114,37 +127,67 @@
     def slab_of(i, which):
         return (i % 2) * per_core + which * per_half + i // 2
 
+    def forward(sems, slot, slab, where):
+        ref = wbuf.at[slot, rows(slab)]
+        return remote(ref, ref, sems.at[slot, slab], w_recv.at[slot, slab], where)
+
     def landed(slot, slab):
-        remote(
-            wbuf.at[slot, rows(slab)], wbuf.at[slot, rows(slab)],
-            w_next.at[slot, slab], w_recv.at[slot, slab], (group, dp, other),
-        ).wait_recv()
-
-    def next_copy(slot, slab, step):
-        return remote(
-            wbuf.at[slot, rows(slab)], wbuf.at[slot, rows(slab)],
-            w_next.at[slot, slab], w_recv.at[slot, slab], (group, dp + 2 * step, core),
-        )
-
-    def side_copy(slot, slab):
-        return remote(
-            wbuf.at[slot, rows(slab)], wbuf.at[slot, rows(slab)],
-            w_side.at[slot, slab], w_recv.at[slot, slab], (cousin, dp, core),
-        )
-
-    def pass_on(slot, origin, i):
-        slab = slab_of(i, half)
-        landed(slot, slab)
-
-        @pl.when(jnp.logical_and(origin < z, z < line - 1))
-        def _():
-            next_copy(slot, slab, 1).start()
-
-        @pl.when(jnp.logical_and(origin > z, z > 0))
-        def _():
-            next_copy(slot, slab, -1).start()
-
-        side_copy(slot, slab).start()
+        forward(w_x, slot, slab, (cousin, dp, core)).wait_recv()
+
+    def to_x(slot, slab):
+        return forward(w_x, slot, slab, (cousin, dp, core))
+
+    def to_y(slot, slab):
+        return forward(w_y, slot, slab, (group, beside, core))
+
+    def z_sends(origin, i, act_on):
+        slot, slab = slot_of(origin, y), slab_of(i, half)
+
+        @pl.when(jnp.logical_and(origin < z, z < line - 2))
+        def _():
+            act_on(forward(w_next, slot, slab, (group, dp + 4, core)))
+
+        @pl.when(jnp.logical_and(origin > z, z > 1))
+        def _():
+            act_on(forward(w_next, slot, slab, (group, dp - 4, core)))
+
+        act_on(to_x(slot, slab))
+        act_on(to_y(slot, slab))
+
+    def x_sends(origin, i, act_on):
+        @pl.when(i < over_y)
+        def _():
+            act_on(to_y(slot_of(origin, y), slab_of(i, 1 - half)))
+
+    def y_sends(origin, i, act_on):
+        @pl.when(jnp.logical_or(origin == z, i >= over_y))
+        def _():
+            act_on(to_x(slot_of(origin, 1 - y), slab_of(i, half)))
+
+    def start(copy):
+        copy.start()
+
+    def z_step(origin, i):
+        landed(slot_of(origin, y), slab_of(i, half))
+        z_sends(origin, i, start)
+
+    def xy_step(origin, i):
+        landed(slot_of(origin, y), slab_of(i, 1 - half))
+        x_sends(origin, i, start)
+        y_step(origin, i)
+
+    def y_step(origin, i):
+        landed(slot_of(origin, 1 - y), slab_of(i, half))
+        y_sends(origin, i, start)
+
+    def origin_of(p):
+        low = core * span
+        inside = low + (z - low + 2 * p + span * line) % span
+        near = low + parity + 2 * p
+        far = low + span - 2 + parity - 2 * p
+        return jnp.where(z < low, near, jnp.where(z >= low + span, far, inside))
+
+    first = origin_of(0)
 
     length = len_ref[dp]
     cached = table_ref.shape[1] * PAGE_TOKENS
@@ -209,13 +252,17 @@
             ).astype(jnp.bfloat16)
         act_copy(i, True).start()
         act_copy(i, False).start()
-        for side in (-1, 1):
-            origin = z + side
-
-            @pl.when(jnp.logical_and(
-                jnp.logical_and(origin >= core * shards, origin < (core + 1) * shards), True))
-            def _():
-                pass_on(origin - core * shards, origin, i)
+        @pl.when(core == own_core)
+        def _():
+            y_step(z, i)
+
+        @pl.when(jnp.logical_and(core != own_core, i % 2 == 1))
+        def _():
+            z_step(first, i // 2)
+
+        @pl.when(jnp.logical_and(core != own_core, jnp.logical_and(i % 2 == 0, i > 0)))
+        def _():
+            xy_step(first, i // 2 - 1)
 
         @pl.when(i >= lag)
         def _():
@@ -227,14 +274,9 @@
     for i in range(per_core - lag, per_core):
         relay(i)
 
-    def origin_of(p):
-        low = core * shards
-        inside = low + (z - low + p + shards * line) % shards
-        return jnp.where(z < low, low + p, jnp.where(z >= low + shards, low + shards - 1 - p, inside))
-
-    def out_cols(origin, n):
-        start = (origin * 2 + y - core * 2 * shards) * cols + n * tile
-        return pl.ds(pl.multiple_of(start, 128), tile)
+    def out_cols(origin, side, n):
+        start_col = (origin % span * 2 + side) * cols + n * tile
+        return pl.ds(pl.multiple_of(start_col, 128), tile)
 
     def out_copy(slot, n, column):
         return remote(
@@ -248,33 +290,25 @@
             preferred_element_type=jnp.float32,
         ).astype(jnp.bfloat16)
 
-    def piece(origin, m):
-        slot = origin - core * shards
-        n = m % tiles
-        column = out_cols(origin, n)
-
-        @pl.when(m < tiles)
-        def _():
-            stage[slot, n] = product(1, slot, n)
-            out_copy(slot, n, column).start()
-
-        @pl.when(m >= tiles)
-        def _():
-            out_ref[:, column] = product(0, slot, n)
-
-    def rest_landed(origin):
-        slot = origin - core * shards
-
-        def one(i, carry):
-            landed(slot, slab_of(i, 1 - half))
-
-            @pl.when(origin == z)
-            def _():
-                landed(slot, slab_of(i, half))
+    def project(origin, side):
+        slot = slot_of(origin, side)
+
+        def piece(m, carry):
+            n = m % tiles
+            column = out_cols(origin, side, n)
+
+            @pl.when(m < tiles)
+            def _():
+                stage[slot, n] = product(1, slot, n)
+                out_copy(slot, n, column).start()
+
+            @pl.when(m >= tiles)
+            def _():
+                out_ref[:, column] = product(0, slot, n)
 
             return carry
 
-        lax.fori_loop(0, per_core, one, 0)
+        lax.fori_loop(0, 2 * tiles, piece, 0)
 
     def acts_landed():
         def one(i, carry):
@@ -284,68 +318,72 @@
 
         lax.fori_loop(0, per_core, one, 0)
 
-    def shard_step(p, carry):
+    def plane_step(p, carry):
         origin = origin_of(p)
-        before = origin_of(jnp.maximum(p - 1, 0))
-
-        def chunk_step(i, inner):
-            @pl.when(jnp.logical_or(origin > z + 1, origin < z - 1))
-            def _():
-                pass_on(origin - core * shards, origin, i)
-
-            @pl.when(jnp.logical_and(p > 0, i == 1))
-            def _():
-                @pl.when(p == 1)
-                def _():
-                    acts_landed()
-
-                rest_landed(before)
-
-            @pl.when(jnp.logical_and(jnp.logical_and(p > 0, i % 2 == 1), i // 2 < 2 * tiles))
-            def _():
-                piece(before, i // 2)
+
+        def chunk_step(m, inner):
+            @pl.when(m < per_core)
+            def _():
+                z_step(origin, m)
+
+            @pl.when(m > 0)
+            def _():
+                xy_step(origin, m - 1)
 
             return inner
 
-        lax.fori_loop(0, per_core, chunk_step, 0)
+        @pl.when(origin != z)
+        def _():
+            begin = jnp.where(p == 0, per_half, 0)
+            lax.fori_loop(begin, per_core + 1, chunk_step, 0)
+
+        @pl.when(p == 0)
+        def _():
+            acts_landed()
+
+        def one_own(i, inner):
+            landed(slot_of(origin, y), slab_of(i, 0))
+            landed(slot_of(origin, y), slab_of(i, 1))
+            return inner
+
+        @pl.when(origin == z)
+        def _():
+            lax.fori_loop(0, per_core, one_own, 0)
+
+        project(origin, y)
+
+        def one(i, inner):
+            landed(slot_of(origin, 1 - y), slab_of(i, 1 - half))
+            return inner
+
+        lax.fori_loop(0, per_core, one, 0)
+        project(origin, 1 - y)
         return carry
 
-    lax.fori_loop(0, shards, shard_step, 0)
-    if shards == 1:
-        acts_landed()
-    last = origin_of(shards - 1)
-    rest_landed(last)
-    lax.fori_loop(0, 2 * tiles, lambda m, carry: (piece(last, m), carry)[1], 0)
-
-    def finish(slot, carry):
-        origin = core * shards + slot
-        for n in range(tiles):
-            start = (origin * 2 + 1 - y - core * 2 * shards) * cols + n * tile
-            copy = out_copy(slot, n, pl.ds(pl.multiple_of(start, 128), tile))
-            copy.wait_recv()
-            copy.wait_send()
-
-        @pl.when(origin != z)
-        def _():
-            def one(i, inner):
-                slab = slab_of(i, half)
-
-                @pl.when(jnp.logical_and(origin < z, z < line - 1))
-                def _():
-                    next_copy(slot, slab, 1).wait_send()
-
-                @pl.when(jnp.logical_and(origin > z, z > 0))
-                def _():
-                    next_copy(slot, slab, -1).wait_send()
-
-                side_copy(slot, slab).wait_send()
-                return inner
-
-            lax.fori_loop(0, per_core, one, 0)
-
+    lax.fori_loop(0, planes, plane_step, 0)
+
+    def finish(index, carry):
+        origin = core * span + index * 2 + parity
+        for side in (0, 1):
+            for n in range(tiles):
+                slot = index * 2 + side
+                copy = out_copy(slot, n, out_cols(origin + 1 - 2 * parity, side, n))
+                copy.wait_recv()
+                copy.wait_send()
+
+        def one(i, inner):
+            @pl.when(origin != z)
+            def _():
+                z_sends(origin, i, lambda copy: copy.wait_send())
+                x_sends(origin, i, lambda copy: copy.wait_send())
+
+            y_sends(origin, i, lambda copy: copy.wait_send())
+            return inner
+
+        lax.fori_loop(0, per_core, one, 0)
         return carry
 
-    lax.fori_loop(0, shards, finish, 0)
+    lax.fori_loop(0, planes, finish, 0)
 
     def acts_sent(i, carry):
         act_copy(i, True).wait_send()
@@ -387,7 +425,8 @@
             dma((shards, 2 * per_core)),
             dma((shards, 2 * per_core)),
             dma((shards, 2 * per_core)),
-            dma((3, per_core)),
+            dma((shards, 2 * per_core)),
+            dma((4, per_core)),
             dma((2, 2 * per_core)),
             dma((2, per_core)),
             dma((per_core,)),

time: 95.3 us -> 103 us (1.081)
  the two profiles are of different devices: /device:TPU:24 before, /device:TPU:16 now
where the time goes in v2:
time: 103 us
  Pallas kernels  101 us (98%)
  local copies, waits for them, and re-layouts  2.3 us (2%)
    pallas_call x1, Pallas kernels, shards_program(): pl.pallas_call(functools.partial(kernel, line), out_shape=jax.ShapeDtypeS...  101 us
    unnamed x1, local copies, waits for them, and re-layouts  2.3 us

profile of v2, /device:TPU:16, one launch (start us, length us, event | category | flops | bytes accessed | tf_op | source)
XLA Modules:
  0.0 102.9 jit_solution(3411532161941060497)
XLA Ops:
  0.0 100.6 %shard_map.82 = bf16[256,2048]{1,0:T(8,128)(2,1)} custom-call(bf16[256,2048]{1,0:T(8,128)(2,1)} %q_ref.1, bf16[256,256]{1,0:T(8,128)(2,1)} %fk_ref.1, bf16[256,256]{1,0:T(8,128)(2,1)} %fv_ref.1, bf16[10,128,256]{2,1,0:T(8,128)(2,1)} %kp_ref.1, bf16[10,128,256]{2,1,0:T(8,128)(2,1)} %vp_ref.1, s32[1,8]{1,0:T(1,128)} %table_ref.1, s32[8]{0:T(128)} %len_ref.1, ...), custom_call_target="tpu_custom_call" | custom-call | flops 6979321856 | bytes 8388608 | tf_op jit(solution)/shard_map/pallas_call | solution.py:413
  100.6 2.3 %copy.10 = bf16[256,2048]{1,0:T(8,128)(2,1)} copy(bf16[256,2048]{1,0:T(8,128)(2,1)} %shard_map.82) | data formatting | bytes 2097152

commit v3 on v1

--- a/solution.py
+++ b/solution.py
@@ -293,21 +293,19 @@
             def _():
                 pass_on(origin - core * shards, origin, i)
 
-            @pl.when(jnp.logical_and(p > 0, i == 1))
-            def _():
-                @pl.when(p == 1)
-                def _():
-                    acts_landed()
-
-                rest_landed(before)
-
-            @pl.when(jnp.logical_and(jnp.logical_and(p > 0, i % 2 == 1), i // 2 < 2 * tiles))
-            def _():
-                piece(before, i // 2)
-
             return inner
 
         lax.fori_loop(0, per_core, chunk_step, 0)
+
+        @pl.when(p > 0)
+        def _():
+            @pl.when(p == 1)
+            def _():
+                acts_landed()
+
+            rest_landed(before)
+            lax.fori_loop(0, 2 * tiles, lambda m, inner: (piece(before, m), inner)[1], 0)
+
         return carry
 
     lax.fori_loop(0, shards, shard_step, 0)

time: 95.3 us -> 94.6 us (level); the launches traced: 95.1 us -> 92.9 us
  Pallas kernels: 92.8 us -> 90.6 us
    pallas_call x1, Pallas kernels: 92.8 us -> 90.6 us  [shards_program(): pl.pallas_call(functools.partial(kernel, line), out_shape=jax.ShapeDtypeS...]
where the time goes in v3:
time: 94.6 us; the launch traced here: 92.9 us
  Pallas kernels  90.6 us (96%)
  local copies, waits for them, and re-layouts  2.3 us (2%)
    pallas_call x1, Pallas kernels, shards_program(): pl.pallas_call(functools.partial(kernel, line), out_shape=jax.ShapeDtypeS...  90.6 us
    unnamed x1, local copies, waits for them, and re-layouts  2.3 us

profile of v3, /device:TPU:24, one launch (start us, length us, event | category | flops | bytes accessed | tf_op | source)
XLA Modules:
  0.0 92.9 jit_solution(5732694691598888475)
XLA Ops:
  0.0 90.6 %shard_map.82 = bf16[256,2048]{1,0:T(8,128)(2,1)} custom-call(bf16[256,2048]{1,0:T(8,128)(2,1)} %q_ref.1, bf16[256,256]{1,0:T(8,128)(2,1)} %fk_ref.1, bf16[256,256]{1,0:T(8,128)(2,1)} %fv_ref.1, bf16[10,128,256]{2,1,0:T(8,128)(2,1)} %kp_ref.1, bf16[10,128,256]{2,1,0:T(8,128)(2,1)} %vp_ref.1, s32[1,8]{1,0:T(1,128)} %table_ref.1, s32[8]{0:T(128)} %len_ref.1, ...), custom_call_target="tpu_custom_call" | custom-call | flops 6979321856 | bytes 8388608 | tf_op jit(solution)/shard_map/pallas_call | solution.py:373
  90.6 2.3 %copy.10 = bf16[256,2048]{1,0:T(8,128)(2,1)} copy(bf16[256,2048]{1,0:T(8,128)(2,1)} %shard_map.82) | data formatting | bytes 2097152
